TPU v7x, 32 devices: a whole 2x2x4 slice. The times are simulated.
32 devices in a mesh: groups: 2 (over y), patch: 4 (over z), sub: 2 (over x), half: 2 (over core).
Axes of the slice: x: 2, y: 2, z: 4, core: 2. Of those that a mesh axis runs over, the one named last changes fastest.
Arguments:
- vectors: float32 [2, 8192, 256], P(None, ('groups', 'patch', 'sub', 'half')), parts along dimension 1, may hold values from -600 to 600
- prestress: bfloat16 [8192, 3, 256], P(('groups', 'patch', 'sub', 'half')), parts along dimension 0, may hold values from -4 to 4
- thickness: float32 [8192, 256], P(('groups', 'patch', 'sub', 'half')), parts along dimension 0, may hold values from 0.5 to 2
- foundation: float32 [8192, 256], P(('groups', 'patch', 'sub', 'half')), parts along dimension 0, may hold values from 2 to 6
- patch_rows: int32 [64], P(('groups', 'patch', 'sub', 'half')), parts along dimension 0, may hold values from 64 to 128, as said below
- matched: int32 [64], P(('groups', 'patch', 'sub', 'half')), parts along dimension 0, may hold values from 0 to 31, as said below
- elem_row: int32 [8192], P(('groups', 'patch', 'sub', 'half')), parts along dimension 0, may hold values from 0 to 4095, as said below
Outputs:
- modes: float32 [2, 8192, 256], P(None, ('groups', 'patch', 'sub', 'half')), parts along dimension 1
There are 2 independent parts, one for each index of `groups`. A program takes and returns all parts, laid end to end along the dimension named above; each array names one. Nothing has to cross between parts.
Inputs may be any that keep to these rules, and one draw needn't show every extreme that they name: `patch_rows`: the largest value is reached by some patch in every draw. A permutation of the patches; the patch matched to a patch lies on the device with the same sub and half indices and a patch index one above or one below, cyclically. `elem_row`: a permutation of the rows; of each device's rows, those in positions k * 16 to (k + 1) * 16 - 1 belong to patches of the device with index k along patch+sub+half.
All inputs are finite; a program needn't handle non-finite values.
Results may differ from a plain program's by a relative error of at most 0.0003.
Values may be sent and summed in bfloat16 or wider, within the bound.
A program may use at most 64 MiB of HBM per device.

v0:
```python
import jax
import jax.numpy as jnp
from jax import lax
from jax.sharding import PartitionSpec as P

ITERS = 2
step_size = 1.0
norm_scale = 16.0
penalty_value = 8.0
penalty_slope = 4.0


def passed_along(array, axis, by):
    peers = lax.axis_size(axis)
    return lax.ppermute(array, axis, [(i, (i + by) % peers) for i in range(peers)])


def second_rows(field):
    padded = jnp.pad(field, [(0, 0)] * (field.ndim - 2) + [(1, 1), (0, 0)])
    return padded[..., :-2, :] - 2.0 * field + padded[..., 2:, :]


def second_cols(field):
    padded = jnp.pad(field, [(0, 0)] * (field.ndim - 1) + [(1, 1)])
    return padded[..., :-2] - 2.0 * field + padded[..., 2:]


def forward_rows(field):
    zeros = jnp.zeros_like(field[..., :1, :])
    return jnp.concatenate([field[..., 1:, :], zeros], axis=-2) - field


def backward_rows(field):
    zeros = jnp.zeros_like(field[..., :1, :])
    return jnp.concatenate([zeros, field[..., :-1, :]], axis=-2) - field


def forward_cols(field):
    zeros = jnp.zeros_like(field[..., :1])
    return jnp.concatenate([field[..., 1:], zeros], axis=-1) - field


def backward_cols(field):
    zeros = jnp.zeros_like(field[..., :1])
    return jnp.concatenate([zeros, field[..., :-1]], axis=-1) - field


def stiffness(field, live, thickness, foundation):
    bend_rows = thickness * live * second_rows(field)
    bend_cols = thickness * second_cols(field)
    return live * (foundation * field + second_rows(bend_rows) + second_cols(bend_cols))


def geometric(field, live, stress):
    along_rows = forward_rows(field)
    along_cols = forward_cols(field)
    nuu = stress[:, :, 0, :]
    nvv = stress[:, :, 1, :]
    nuv = stress[:, :, 2, :]
    total = backward_rows(nuu * along_rows + nuv * along_cols) + backward_cols(
        nvv * along_cols + nuv * along_rows
    )
    return live * total


def edges(field, lengths):

    def row_pick(index):
        where_rows = jnp.broadcast_to(
            index[None, :, None, None], (field.shape[0], field.shape[1], 1, field.shape[3])
        )
        return jnp.take_along_axis(field, where_rows, axis=2)[:, :, 0, :]

    top = jnp.stack([row_pick(lengths - 2), row_pick(lengths - 1)], axis=2)
    bottom = field[:, :, 0:2, :]
    return (top, bottom)


def interface(field, lengths, top, bottom, partner_top, partner_bottom):
    jump_top = top[:, :, 1, :] - partner_bottom[:, :, 0, :]
    slope_top = (
        top[:, :, 1, :]
        - top[:, :, 0, :]
        - (partner_bottom[:, :, 1, :] - partner_bottom[:, :, 0, :])
    )
    jump_bottom = partner_top[:, :, 1, :] - bottom[:, :, 0, :]
    slope_bottom = (
        partner_top[:, :, 1, :]
        - partner_top[:, :, 0, :]
        - (bottom[:, :, 1, :] - bottom[:, :, 0, :])
    )
    rows = jnp.arange(field.shape[2], dtype=jnp.int32)[None, :, None]
    last = lengths[:, None, None] - 1
    added = jnp.where(
        rows == last, (penalty_value * jump_top + penalty_slope * slope_top)[:, :, None, :], 0.0
    )
    added = added + jnp.where(rows == last - 1, (-penalty_slope * slope_top)[:, :, None, :], 0.0)
    added = added + jnp.where(
        rows == 0, (-penalty_value * jump_bottom + penalty_slope * slope_bottom)[:, :, None, :], 0.0
    )
    added = added + jnp.where(rows == 1, (-penalty_slope * slope_bottom)[:, :, None, :], 0.0)
    return added


def products(field, kfield, gfield):
    return jnp.stack(
        [
            jnp.sum(field[0] * kfield[0]),
            jnp.sum(field[0] * kfield[1]),
            jnp.sum(field[1] * kfield[1]),
            jnp.sum(field[0] * gfield[0]),
            jnp.sum(field[0] * gfield[1]),
            jnp.sum(field[1] * gfield[1]),
        ]
    )


def advance(field, kfield, gfield, totals, precond, cells):
    first_a = totals[0]
    cross_k = totals[1]
    second_a = totals[2]
    first_g = totals[3]
    cross_g = totals[4]
    second_g = totals[5]
    ratio = cross_k / first_a
    other = field[1] - ratio * field[0]
    other_k = kfield[1] - ratio * kfield[0]
    other_g = gfield[1] - ratio * gfield[0]
    other_a = second_a - ratio * cross_k
    other_q = second_g - 2.0 * ratio * cross_g + ratio * ratio * first_g
    first_mu = first_g / first_a
    other_mu = other_q / other_a
    new_first = (field[0] + step_size * precond * (gfield[0] - first_mu * kfield[0])) * jnp.sqrt(
        norm_scale * cells / first_a
    )
    new_other = (other + step_size * precond * (other_g - other_mu * other_k)) * jnp.sqrt(
        norm_scale * cells / other_a
    )
    return jnp.stack([new_first, new_other])


def choose(candidates, wanted, labels):
    match = labels[None, :] == wanted[:, None]
    return jnp.sum(jnp.where(match[None, :, :, None, None], candidates[:, None], 0.0), axis=2)


def per_device(vectors, prestress, thickness, foundation, patch_rows, matched, elem_row):
    owners = lax.axis_size("patch")
    inner = lax.axis_size(("sub", "half"))
    slots = patch_rows.shape[0]
    rows_dev = thickness.shape[0]
    prows = rows_dev // slots
    ncol = thickness.shape[1]
    per_peer = rows_dev // (owners * inner)
    blocks = prestress.reshape(owners, inner, per_peer, 3, ncol)
    targets = (elem_row % rows_dev).reshape(owners, inner, per_peer)
    arrived, arrived_rows = (
        lax.all_to_all(
            lax.all_to_all(blocks, "patch", split_axis=0, concat_axis=0, tiled=True),
            ("sub", "half"),
            split_axis=1,
            concat_axis=1,
            tiled=True,
        ),
        lax.all_to_all(
            lax.all_to_all(targets, "patch", split_axis=0, concat_axis=0, tiled=True),
            ("sub", "half"),
            split_axis=1,
            concat_axis=1,
            tiled=True,
        ),
    )
    placed = (
        jnp.zeros((rows_dev, 3, ncol), jnp.bfloat16)
        .at[arrived_rows.reshape(-1)]
        .set(arrived.reshape(-1, 3, ncol))
    )
    stress = placed.astype(jnp.float32).reshape(slots, prows, 3, ncol)
    rows = jnp.arange(prows, dtype=jnp.int32)[None, :]
    live = (rows < patch_rows[:, None]).astype(jnp.float32)[:, :, None]
    thick = thickness.reshape(slots, prows, ncol)
    support = foundation.reshape(slots, prows, ncol)
    precond = live / (support + 12.0 * thick)
    own_ids = lax.axis_index(("patch", "sub", "half")) * slots + jnp.arange(slots, dtype=jnp.int32)
    labels = jnp.stack([own_ids, matched])
    field = vectors.reshape(2, slots, prows, ncol) * live
    cells = jnp.float32(owners * inner * rows_dev * ncol)
    for step in range(ITERS):
        top, bottom = edges(field, patch_rows)
        strips = jnp.stack([top, bottom])
        below = passed_along((strips, labels), "patch", 1)
        above = passed_along((strips, labels), "patch", -1)
        got_strips = jnp.stack([below[0], above[0]])
        got_labels = jnp.stack([below[1], above[1]])
        count = got_strips.shape[0] * slots
        cand_top = jnp.moveaxis(got_strips[:, 0], 0, 1).reshape(2, count, 2, ncol)
        cand_bottom = jnp.moveaxis(got_strips[:, 1], 0, 1).reshape(2, count, 2, ncol)
        cand_ids = got_labels[:, 0].reshape(-1)
        cand_next = got_labels[:, 1].reshape(-1)
        partner_bottom = choose(cand_bottom, matched, cand_ids)
        partner_top = choose(cand_top, own_ids, cand_next)
        kfield = stiffness(field, live, thick, support) + interface(
            field, patch_rows, top, bottom, partner_top, partner_bottom
        )
        gfield = geometric(field, live, stress)
        totals = lax.psum(products(field, kfield, gfield), ("patch", "sub", "half"))
        field = advance(field, kfield, gfield, totals, precond, cells)
    return field.reshape(2, rows_dev, ncol)


def solution(mesh):
    in_specs = (
        P(None, ("groups", "patch", "sub", "half"), None),
        P(("groups", "patch", "sub", "half"), None, None),
        P(("groups", "patch", "sub", "half"), None),
        P(("groups", "patch", "sub", "half"), None),
        P(("groups", "patch", "sub", "half")),
        P(("groups", "patch", "sub", "half")),
        P(("groups", "patch", "sub", "half")),
    )
    out_specs = P(None, ("groups", "patch", "sub", "half"), None)
    return jax.shard_map(
        per_device, mesh=mesh, in_specs=in_specs, out_specs=out_specs, check_vma=False
    )
```

profile of v0, /device:TPU:0, one launch (start us, length us, event | category | flops | bytes accessed | tf_op | source)
XLA Modules:
  0.0 211.1 jit_solution(15988298672852159609)
XLA Ops:
  0.0 0.7 broadcast_add_fusion
  1.1 1.1 broadcast_multiply_fusion
  2.2 12.3 %gather_fusion = f32[1024]{0:T(1024)S(1)} fusion(f32[2,2,128,256]{3,2,1,0:T(8,128)S(1)} %broadcast_multiply_fusion, s32[1024]{0:T(1024)S(1)} %bitcast.210), kind=kCustom, calls=%fused_computation.clone | custom fusion | bytes 24576 | tf_op jit(solution)/shard_map/jit(take_along_axis)/gather | solution.py:72
  14.6 12.3 %gather_fusion.1 = f32[1024]{0:T(1024)S(1)} fusion(f32[2,2,128,256]{3,2,1,0:T(8,128)S(1)} %broadcast_multiply_fusion, s32[1024]{0:T(1024)S(1)} %bitcast.212), kind=kCustom, calls=%fused_computation.1.clone | custom fusion | bytes 24576 | tf_op jit(solution)/shard_map/jit(take_along_axis)/gather | solution.py:72
  26.9 0.1 broadcast_select_fusion.4
  27.1 3.1 %collective-permute-start.2 = (f32[2,2,2,2,256]{4,3,2,1,0:T(2,128)S(1)}, f32[2,2,2,2,256]{4,3,2,1,0:T(2,128)S(1)}, u32[]{:S(2)}, u32[]{:S(2)}) collective-permute-start(f32[2,2,2,2,256]{4,3,2,1,0:T(2,128)S(1)} %pad_maximum_fusion.4), channel_id=1, source_target_pairs={{0,4},{4,8},{8,12},{12,0},{1,5},{5,9},{9,13},{13,1},{2,6},{6,10},{... | collective-permute-start | bytes 49160 | tf_op jit(solution)/shard_map/ppermute | solution.py:15
  30.1 2.1 collective-permute-start.3
  32.2 0.7 copy-done.13
  33.0 3.8 %collective-permute-start.1 = (s32[2,2]{1,0:T(2,128)S(1)}, s32[2,2]{1,0:T(2,128)S(1)}, u32[]{:S(2)}, u32[]{:S(2)}) collective-permute-start(s32[2,2]{1,0:T(2,128)S(1)} %pad_add_fusion.4), channel_id=1, source_target_pairs={{0,12},{4,0},{8,4},{12,8},{1,13},{5,1},{9,5},{13,9},{2,14},{6,2},{... | collective-permute-start | bytes 56 | tf_op jit(solution)/shard_map/ppermute | solution.py:15
  36.8 0.7 reshape.291
  37.5 3.2 %all-to-all-start = ((s32[4,4,16]{2,1,0:T(4,128)}), s32[4,4,16]{2,1,0:T(4,128)S(1)}, u32[]{:S(2)}, u32[]{:S(2)}) async-start(s32[4,4,16]{2,1,0:T(4,128)} %reshape.291), calls=%async_computation | async-start | bytes 16384 | tf_op jit(solution)/shard_map/all_to_all | solution.py:166
  40.8 1.0 slice.350
  41.9 0.1 broadcast_multiply_fusion.1
  42.0 0.8 copy-done.10
  42.8 0.8 copy.30
  43.6 0.1 eq.61
  43.7 0.1 eq.129
  43.8 2.4 %all-to-all-done = s32[4,4,16]{2,1,0:T(4,128)S(1)} async-done(((s32[4,4,16]{2,1,0:T(4,128)}), s32[4,4,16]{2,1,0:T(4,128)S(1)}, u32[]{:S(2)}, u32[]{:S(2)}) %all-to-all-start) | async-done | bytes 1056 | tf_op jit(solution)/shard_map/all_to_all | solution.py:166
  46.3 0.6 copy.28
  46.9 3.2 %all-to-all-start.1 = ((s32[4,4,16]{2,0,1:T(4,128)}), s32[4,4,16]{2,0,1:T(4,128)S(1)}, u32[]{:S(2)}, u32[]{:S(2)}) async-start(s32[4,4,16]{2,0,1:T(4,128)} %copy.28), calls=%async_computation.1 | async-start | bytes 16384 | tf_op jit(solution)/shard_map/all_to_all | solution.py:165
  50.2 3.7 %all-to-all-done.1 = s32[4,4,16]{2,0,1:T(4,128)S(1)} async-done(((s32[4,4,16]{2,0,1:T(4,128)}), s32[4,4,16]{2,0,1:T(4,128)S(1)}, u32[]{:S(2)}, u32[]{:S(2)}) %all-to-all-start.1) | async-done | bytes 1056 | tf_op jit(solution)/shard_map/all_to_all | solution.py:165
  53.9 3.5 %all-to-all-start.2 = ((bf16[4,4,16,3,256]{4,2,1,3,0:T(8,128)(2,1)}), bf16[4,4,16,3,256]{4,2,1,3,0:T(8,128)(2,1)S(1)}, u32[]{:S(2)}, u32[]{:S(2)}) async-start(bf16[4,4,16,3,256]{4,2,1,3,0:T(8,128)(2,1)} %copy.30), calls=%async_computation.2 | async-start | bytes 786432 | tf_op jit(solution)/shard_map/all_to_all | solution.py:159
  57.4 0.1 reshape.292
  57.5 0.1 select_reduce_fusion.3
  57.6 0.1 select_reduce_fusion.2
  57.8 11.4 %all-to-all-done.2 = bf16[4,4,16,3,256]{4,2,1,3,0:T(8,128)(2,1)S(1)} async-done(((bf16[4,4,16,3,256]{4,2,1,3,0:T(8,128)(2,1)}), bf16[4,4,16,3,256]{4,2,1,3,0:T(8,128)(2,1)S(1)}, u32[]{:S(2)}, u32[]{:S(2)}) %all-to-all-start.2) | async-done | bytes 393248 | tf_op jit(solution)/shard_map/all_to_all | solution.py:159
  69.2 0.8 copy.31
  70.0 3.5 %all-to-all-start.3 = ((bf16[4,4,16,3,256]{4,2,0,3,1:T(8,128)(2,1)}), bf16[4,4,16,3,256]{4,2,0,3,1:T(8,128)(2,1)S(1)}, u32[]{:S(2)}, u32[]{:S(2)}) async-start(bf16[4,4,16,3,256]{4,2,0,3,1:T(8,128)(2,1)} %copy.31), calls=%async_computation.3 | async-start | bytes 786432 | tf_op jit(solution)/shard_map/all_to_all | solution.py:158
  73.6 7.3 %all-to-all-done.3 = bf16[4,4,16,3,256]{4,2,0,3,1:T(8,128)(2,1)S(1)} async-done(((bf16[4,4,16,3,256]{4,2,0,3,1:T(8,128)(2,1)}), bf16[4,4,16,3,256]{4,2,0,3,1:T(8,128)(2,1)S(1)}, u32[]{:S(2)}, u32[]{:S(2)}) %all-to-all-start.3) | async-done | bytes 393248 | tf_op jit(solution)/shard_map/all_to_all | solution.py:158
  80.9 0.3 copy.33
  81.3 0.1 broadcast_in_dim.225
  81.4 7.0 %scatter_fusion = bf16[256,3,256]{2,1,0:T(4,128)(2,1)S(1)} fusion(bf16[256,3,256]{2,1,0:T(4,128)(2,1)S(1)} %broadcast_in_dim.225, s32[256]{0:T(256)S(1)} %bitcast.260, bf16[256,3,256]{2,1,0:T(4,128)(2,1)S(1)} %copy.33), kind=kCustom, calls=%fused_computation.4 | custom fusion | bytes 1180672 | tf_op jit(solution)/shard_map/scatter | solution.py:176
  88.4 0.5 fusion.89
  89.1 1.2 copy-done.7
  90.2 0.5 fusion.20
  90.7 0.5 copy-done.1
  91.2 0.2 copy-done.6
  91.3 0.8 fusion.8
  92.2 0.8 fusion.37
  93.0 3.8 %stack.135 = f32[6]{0:T(128)S(1)} concatenate(f32[1]{0:T(128)} %bitcast.30, f32[1]{0:T(128)} %bitcast.32, f32[1]{0:T(128)} %bitcast.34, f32[1]{0:T(128)} %bitcast.36, f32[1]{0:T(128)} %bitcast.38, f32[1]{0:T(128)} %bitcast.39), dimensions={0} | concatenate | bytes 48 | tf_op jit(solution)/shard_map/stack | solution.py:106
  96.8 30.2 %psum.14 = f32[6]{0:T(128)S(1)} all-reduce(f32[6]{0:T(128)S(1)} %stack.135), channel_id=1, replica_groups=mesh['groups'=2,'patch'=4,'sub'=2,'half'=2] {'patch','sub','half'}, use_global_device_ids=true, to_apply=%region_9.11 | all-reduce | flops 6 | bytes 48 | tf_op jit(solution)/shard_map/psum | solution.py:206
  127.1 0.7 fusion.91
  134.1 1.0 fusion.41
  135.1 0.2 add_multiply_fusion.5
  135.3 0.2 fusion.29
  135.6 0.9 copy-done.3
  136.6 0.2 multiply_add_fusion.1
  136.7 12.3 %gather_fusion.3 = f32[1024]{0:T(1024)S(1)} fusion(f32[2,2,128,256]{3,2,1,0:T(8,128)S(1)} %get-tuple-element.46, s32[1024]{0:T(1024)S(1)} %bitcast.213), kind=kCustom, calls=%fused_computation.3.clone | custom fusion | bytes 24576 | tf_op jit(solution)/shard_map/jit(take_along_axis)/gather | solution.py:72
  149.1 12.3 %gather_fusion.2 = f32[1024]{0:T(1024)S(1)} fusion(f32[2,2,128,256]{3,2,1,0:T(8,128)S(1)} %get-tuple-element.46, s32[1024]{0:T(1024)S(1)} %bitcast.211), kind=kCustom, calls=%fused_computation.2.clone | custom fusion | bytes 24576 | tf_op jit(solution)/shard_map/jit(take_along_axis)/gather | solution.py:72
  161.6 3.8 %collective-permute-start.5 = (f32[2,2,2,2,256]{4,3,2,1,0:T(2,128)S(1)}, f32[2,2,2,2,256]{4,3,2,1,0:T(2,128)S(1)}, u32[]{:S(2)}, u32[]{:S(2)}) collective-permute-start(f32[2,2,2,2,256]{4,3,2,1,0:T(2,128)S(1)} %pad_maximum_fusion.5), channel_id=1, source_target_pairs={{0,12},{4,0},{8,4},{12,8},{1,13},{5,1},{9,5},{13,9},{2,14},{6,2},{... | collective-permute-start | bytes 49160 | tf_op jit(solution)/shard_map/ppermute | solution.py:15
  165.5 0.4 fusion.25
  165.8 0.2 add_multiply_fusion
  166.1 1.1 collective-permute-done.4
  167.2 0.1 select_reduce_fusion.1
  167.3 0.1 multiply_add_fusion.6
  167.5 0.1 select_reduce_fusion
  167.7 0.6 fusion.17
  168.3 0.3 copy-done.8
  168.7 0.8 fusion.33
  169.5 3.8 %stack.150 = f32[6]{0:T(128)S(1)} concatenate(f32[1]{0:T(128)} %bitcast.59, f32[1]{0:T(128)} %bitcast.61, f32[1]{0:T(128)} %bitcast.62, f32[1]{0:T(128)} %bitcast.64, f32[1]{0:T(128)} %bitcast.66, f32[1]{0:T(128)} %bitcast.67), dimensions={0} | concatenate | bytes 48 | tf_op jit(solution)/shard_map/stack | solution.py:106
  173.4 29.5 %psum.15 = f32[6]{0:T(128)S(1)} all-reduce(f32[6]{0:T(128)S(1)} %stack.150), channel_id=1, replica_groups=mesh['groups'=2,'patch'=4,'sub'=2,'half'=2] {'patch','sub','half'}, use_global_device_ids=true, to_apply=%region_18.20 | all-reduce | flops 6 | bytes 48 | tf_op jit(solution)/shard_map/psum | solution.py:206
  202.9 0.7 fusion.90
  210.1 0.2 add_multiply_fusion.3
  210.3 0.8 pad_maximum_fusion.1
  (90 shorter events, 1.5 us)
Async XLA Ops:
  0.0 0.7 copy-start.12
  27.1 30.4 %collective-permute-start.2 = (f32[2,2,2,2,256]{4,3,2,1,0:T(2,128)S(1)}, f32[2,2,2,2,256]{4,3,2,1,0:T(2,128)S(1)}, u32[]{:S(2)}, u32[]{:S(2)}) collective-permute-start(f32[2,2,2,2,256]{4,3,2,1,0:T(2,128)S(1)} %pad_maximum_fusion.4), channel_id=1, source_target_pairs={{0,4},{4,8},{8,12},{12,0},{1,5},{5,9},{9,13},{13,1},{2,6},{6,10},{... | collective-permute-start | bytes 49160 | tf_op jit(solution)/shard_map/ppermute | solution.py:15
  30.1 27.3 %collective-permute-start.3 = (f32[2,2,2,2,256]{4,3,2,1,0:T(2,128)S(1)}, f32[2,2,2,2,256]{4,3,2,1,0:T(2,128)S(1)}, u32[]{:S(2)}, u32[]{:S(2)}) collective-permute-start(f32[2,2,2,2,256]{4,3,2,1,0:T(2,128)S(1)} %pad_maximum_fusion.4), channel_id=1, source_target_pairs={{0,12},{4,0},{8,4},{12,8},{1,13},{5,1},{9,5},{13,9},{2,14},{6,2},{... | collective-permute-start | bytes 49160 | tf_op jit(solution)/shard_map/ppermute | solution.py:15
  32.2 0.7 copy-start.13
  32.9 3.9 %copy-start.11 = (s32[256]{0:T(256)S(1)}, s32[256]{0:T(256)}, u32[]{:S(2)}) copy-start(s32[256]{0:T(256)} %param.15) | copy-start | bytes 3076
  32.9 10.7 %collective-permute-start = (s32[2,2]{1,0:T(2,128)S(1)}, s32[2,2]{1,0:T(2,128)S(1)}, u32[]{:S(2)}, u32[]{:S(2)}) collective-permute-start(s32[2,2]{1,0:T(2,128)S(1)} %pad_add_fusion.4), channel_id=1, source_target_pairs={{0,4},{4,8},{8,12},{12,0},{1,5},{5,9},{9,13},{13,1},{2,6},{6,10},{... | collective-permute-start | bytes 56 | tf_op jit(solution)/shard_map/ppermute | solution.py:15
  33.0 10.6 %collective-permute-start.1 = (s32[2,2]{1,0:T(2,128)S(1)}, s32[2,2]{1,0:T(2,128)S(1)}, u32[]{:S(2)}, u32[]{:S(2)}) collective-permute-start(s32[2,2]{1,0:T(2,128)S(1)} %pad_add_fusion.4), channel_id=1, source_target_pairs={{0,12},{4,0},{8,4},{12,8},{1,13},{5,1},{9,5},{13,9},{2,14},{6,2},{... | collective-permute-start | bytes 56 | tf_op jit(solution)/shard_map/ppermute | solution.py:15
  37.5 8.8 %all-to-all-start = ((s32[4,4,16]{2,1,0:T(4,128)}), s32[4,4,16]{2,1,0:T(4,128)S(1)}, u32[]{:S(2)}, u32[]{:S(2)}) async-start(s32[4,4,16]{2,1,0:T(4,128)} %reshape.291), calls=%async_computation | async-start | bytes 16384 | tf_op jit(solution)/shard_map/all_to_all | solution.py:166
  40.8 1.1 copy-start
  41.8 1.0 copy-start.10
  46.9 7.0 %all-to-all-start.1 = ((s32[4,4,16]{2,0,1:T(4,128)}), s32[4,4,16]{2,0,1:T(4,128)S(1)}, u32[]{:S(2)}, u32[]{:S(2)}) async-start(s32[4,4,16]{2,0,1:T(4,128)} %copy.28), calls=%async_computation.1 | async-start | bytes 16384 | tf_op jit(solution)/shard_map/all_to_all | solution.py:165
  53.9 15.4 %all-to-all-start.2 = ((bf16[4,4,16,3,256]{4,2,1,3,0:T(8,128)(2,1)}), bf16[4,4,16,3,256]{4,2,1,3,0:T(8,128)(2,1)S(1)}, u32[]{:S(2)}, u32[]{:S(2)}) async-start(bf16[4,4,16,3,256]{4,2,1,3,0:T(8,128)(2,1)} %copy.30), calls=%async_computation.2 | async-start | bytes 786432 | tf_op jit(solution)/shard_map/all_to_all | solution.py:159
  70.0 10.9 %all-to-all-start.3 = ((bf16[4,4,16,3,256]{4,2,0,3,1:T(8,128)(2,1)}), bf16[4,4,16,3,256]{4,2,0,3,1:T(8,128)(2,1)S(1)}, u32[]{:S(2)}, u32[]{:S(2)}) async-start(bf16[4,4,16,3,256]{4,2,0,3,1:T(8,128)(2,1)} %copy.31), calls=%async_computation.3 | async-start | bytes 786432 | tf_op jit(solution)/shard_map/all_to_all | solution.py:158
  89.0 1.2 copy-start.7
  89.0 1.6 copy-start.2
  89.0 1.6 copy-start.4
  90.2 0.9 copy-start.1
  90.2 1.1 copy-start.6
  135.5 1.0 copy-start.3
  135.5 1.0 copy-start.5
  161.6 5.6 %collective-permute-start.4 = (f32[2,2,2,2,256]{4,3,2,1,0:T(2,128)S(1)}, f32[2,2,2,2,256]{4,3,2,1,0:T(2,128)S(1)}, u32[]{:S(2)}, u32[]{:S(2)}) collective-permute-start(f32[2,2,2,2,256]{4,3,2,1,0:T(2,128)S(1)} %pad_maximum_fusion.5), channel_id=1, source_target_pairs={{0,4},{4,8},{8,12},{12,0},{1,5},{5,9},{9,13},{13,1},{2,6},{6,10},{... | collective-permute-start | bytes 49160 | tf_op jit(solution)/shard_map/ppermute | solution.py:15
  161.6 5.5 %collective-permute-start.5 = (f32[2,2,2,2,256]{4,3,2,1,0:T(2,128)S(1)}, f32[2,2,2,2,256]{4,3,2,1,0:T(2,128)S(1)}, u32[]{:S(2)}, u32[]{:S(2)}) collective-permute-start(f32[2,2,2,2,256]{4,3,2,1,0:T(2,128)S(1)} %pad_maximum_fusion.5), channel_id=1, source_target_pairs={{0,12},{4,0},{8,4},{12,8},{1,13},{5,1},{9,5},{13,9},{2,14},{6,2},{... | collective-permute-start | bytes 49160 | tf_op jit(solution)/shard_map/ppermute | solution.py:15
  167.6 1.0 copy-start.8
  167.7 1.0 copy-start.9
where the time goes:
time: 212 us; the launch traced here: 211 us
  local copies, waits for them, and re-layouts  75.2 us (35%)
  blocking collectives  59.7 us (28%)
  starting transfers between devices  26.3 us (12%)
  waiting for transfers between devices  26 us (12%)
  between operations  13.6 us (6%)
  other arithmetic  10.3 us (5%)
    psum x2, blocking collectives, per_device(): totals = lax.psum(products(field, kfield, gfield), ('patch', 'sub', 'half'))  59.7 us
    gather x4, local copies, waits for them, and re-layouts, row_pick(): return jnp.take_along_axis(field, where_rows, axis=2)[:, :, 0, :]  49.2 us
    ppermute x6, starting transfers between devices, passed_along(): lax.ppermute(array, axis, [(i, (i + by) % peers) for i in range(peers)])  12.9 us
    all_to_all x1, waiting for transfers between devices, per_device(): lax.all_to_all(blocks, 'patch', split_axis=0, concat_axis=0, tiled=True)  11.4 us
    another operation x2, local copies, waits for them, and re-layouts, products(): jnp.stack([jnp.sum(field[0] * kfield[0]), jnp.sum(field[0] * kfield[1]),...  7.63 us
    all_to_all x1, waiting for transfers between devices, per_device(): lax.all_to_all(lax.all_to_all(blocks, 'patch', split_axis=0, concat_axis=...  7.33 us
    scatter x1, local copies, waits for them, and re-layouts, per_device(): placed = jnp.zeros((rows_dev, 3, ncol), jnp.bfloat16).at[arrived_rows.res...  6.97 us
    unnamed x40, local copies, waits for them, and re-layouts  4.77 us
  transfers between devices with their start and end apart: 10, of which 5 were waited for; matrix products, arithmetic and copies ran while one was open for 2% of the time, Pallas kernels for 0%

commit v1 on v0

--- a/solution.py
+++ b/solution.py
@@ -203,7 +203,9 @@
             field, patch_rows, top, bottom, partner_top, partner_bottom
         )
         gfield = geometric(field, live, stress)
-        totals = lax.psum(products(field, kfield, gfield), ("patch", "sub", "half"))
+        totals = products(field, kfield, gfield)
+        for mesh_axis in (("sub", "half"), "patch"):
+            totals = lax.psum(totals, mesh_axis)
         field = advance(field, kfield, gfield, totals, precond, cells)
     return field.reshape(2, rows_dev, ncol)
 

time: 212 us -> 186 us (0.88)
  blocking collectives: 59.7 us -> 33.4 us
    psum x2 -> x4, blocking collectives: 59.7 us -> 33.4 us  [per_device(): totals = lax.psum(totals, mesh_axis)]
  transfers between devices with their start and end apart: 10 -> 10, of which waited for: 5 -> 5; matrix products, arithmetic and copies ran while one was open for 2% -> 3% of each run, Pallas kernels for 0% -> 0%
where the time goes in v1:
time: 186 us; the launch traced here: 185 us
  local copies, waits for them, and re-layouts  75.2 us (40%)
  blocking collectives  33.4 us (18%)
  starting transfers between devices  26.3 us (14%)
  waiting for transfers between devices  26 us (14%)
  between operations  13.6 us (7%)
  other arithmetic  10.3 us (6%)
    gather x4, local copies, waits for them, and re-layouts, row_pick(): return jnp.take_along_axis(field, where_rows, axis=2)[:, :, 0, :]  49.2 us
    psum x4, blocking collectives, per_device(): totals = lax.psum(totals, mesh_axis)  33.4 us
    ppermute x6, starting transfers between devices, passed_along(): lax.ppermute(array, axis, [(i, (i + by) % peers) for i in range(peers)])  12.9 us
    all_to_all x1, waiting for transfers between devices, per_device(): lax.all_to_all(blocks, 'patch', split_axis=0, concat_axis=0, tiled=True)  11.4 us
    another operation x2, local copies, waits for them, and re-layouts, products(): jnp.stack([jnp.sum(field[0] * kfield[0]), jnp.sum(field[0] * kfield[1]),...  7.63 us
    all_to_all x1, waiting for transfers between devices, per_device(): lax.all_to_all(lax.all_to_all(blocks, 'patch', split_axis=0, concat_axis=...  7.33 us
    scatter x1, local copies, waits for them, and re-layouts, per_device(): placed = jnp.zeros((rows_dev, 3, ncol), jnp.bfloat16).at[arrived_rows.res...  6.97 us
    unnamed x40, local copies, waits for them, and re-layouts  4.77 us
  transfers between devices with their start and end apart: 10, of which 5 were waited for; matrix products, arithmetic and copies ran while one was open for 3% of the time, Pallas kernels for 0%

profile of v1, /device:TPU:0, one launch (start us, length us, event | category | flops | bytes accessed | tf_op | source)
XLA Modules:
  0.0 184.7 jit_solution(1604891253393399544)
XLA Ops:
  0.0 0.7 broadcast_add_fusion
  1.1 1.1 broadcast_multiply_fusion
  2.2 12.3 %gather_fusion = f32[1024]{0:T(1024)S(1)} fusion(f32[2,2,128,256]{3,2,1,0:T(8,128)S(1)} %broadcast_multiply_fusion, s32[1024]{0:T(1024)S(1)} %bitcast.210), kind=kCustom, calls=%fused_computation.clone | custom fusion | bytes 24576 | tf_op jit(solution)/shard_map/jit(take_along_axis)/gather | solution.py:72
  14.6 12.3 %gather_fusion.1 = f32[1024]{0:T(1024)S(1)} fusion(f32[2,2,128,256]{3,2,1,0:T(8,128)S(1)} %broadcast_multiply_fusion, s32[1024]{0:T(1024)S(1)} %bitcast.212), kind=kCustom, calls=%fused_computation.1.clone | custom fusion | bytes 24576 | tf_op jit(solution)/shard_map/jit(take_along_axis)/gather | solution.py:72
  27.1 3.1 %collective-permute-start.2 = (f32[2,2,2,2,256]{4,3,2,1,0:T(2,128)S(1)}, f32[2,2,2,2,256]{4,3,2,1,0:T(2,128)S(1)}, u32[]{:S(2)}, u32[]{:S(2)}) collective-permute-start(f32[2,2,2,2,256]{4,3,2,1,0:T(2,128)S(1)} %pad_maximum_fusion.4), channel_id=1, source_target_pairs={{0,4},{4,8},{8,12},{12,0},{1,5},{5,9},{9,13},{13,1},{2,6},{6,10},{... | collective-permute-start | bytes 49160 | tf_op jit(solution)/shard_map/ppermute | solution.py:15
  30.1 2.1 %collective-permute-start.3 = (f32[2,2,2,2,256]{4,3,2,1,0:T(2,128)S(1)}, f32[2,2,2,2,256]{4,3,2,1,0:T(2,128)S(1)}, u32[]{:S(2)}, u32[]{:S(2)}) collective-permute-start(f32[2,2,2,2,256]{4,3,2,1,0:T(2,128)S(1)} %pad_maximum_fusion.4), channel_id=1, source_target_pairs={{0,12},{4,0},{8,4},{12,8},{1,13},{5,1},{9,5},{13,9},{2,14},{6,2},{... | collective-permute-start | bytes 49160 | tf_op jit(solution)/shard_map/ppermute | solution.py:15
  32.2 0.7 copy-done.13
  33.0 3.8 %collective-permute-start.1 = (s32[2,2]{1,0:T(2,128)S(1)}, s32[2,2]{1,0:T(2,128)S(1)}, u32[]{:S(2)}, u32[]{:S(2)}) collective-permute-start(s32[2,2]{1,0:T(2,128)S(1)} %pad_add_fusion.4), channel_id=1, source_target_pairs={{0,12},{4,0},{8,4},{12,8},{1,13},{5,1},{9,5},{13,9},{2,14},{6,2},{... | collective-permute-start | bytes 56 | tf_op jit(solution)/shard_map/ppermute | solution.py:15
  36.8 0.7 reshape.291
  37.5 3.2 %all-to-all-start = ((s32[4,4,16]{2,1,0:T(4,128)}), s32[4,4,16]{2,1,0:T(4,128)S(1)}, u32[]{:S(2)}, u32[]{:S(2)}) async-start(s32[4,4,16]{2,1,0:T(4,128)} %reshape.291), calls=%async_computation | async-start | bytes 16384 | tf_op jit(solution)/shard_map/all_to_all | solution.py:166
  40.8 1.0 slice.350
  41.9 0.1 broadcast_multiply_fusion.1
  42.0 0.8 copy-done.10
  42.8 0.8 copy.30
  43.8 2.4 %all-to-all-done = s32[4,4,16]{2,1,0:T(4,128)S(1)} async-done(((s32[4,4,16]{2,1,0:T(4,128)}), s32[4,4,16]{2,1,0:T(4,128)S(1)}, u32[]{:S(2)}, u32[]{:S(2)}) %all-to-all-start) | async-done | bytes 1056 | tf_op jit(solution)/shard_map/all_to_all | solution.py:166
  46.3 0.6 copy.28
  46.9 3.2 %all-to-all-start.1 = ((s32[4,4,16]{2,0,1:T(4,128)}), s32[4,4,16]{2,0,1:T(4,128)S(1)}, u32[]{:S(2)}, u32[]{:S(2)}) async-start(s32[4,4,16]{2,0,1:T(4,128)} %copy.28), calls=%async_computation.1 | async-start | bytes 16384 | tf_op jit(solution)/shard_map/all_to_all | solution.py:165
  50.2 3.7 %all-to-all-done.1 = s32[4,4,16]{2,0,1:T(4,128)S(1)} async-done(((s32[4,4,16]{2,0,1:T(4,128)}), s32[4,4,16]{2,0,1:T(4,128)S(1)}, u32[]{:S(2)}, u32[]{:S(2)}) %all-to-all-start.1) | async-done | bytes 1056 | tf_op jit(solution)/shard_map/all_to_all | solution.py:165
  53.9 3.5 %all-to-all-start.2 = ((bf16[4,4,16,3,256]{4,2,1,3,0:T(8,128)(2,1)}), bf16[4,4,16,3,256]{4,2,1,3,0:T(8,128)(2,1)S(1)}, u32[]{:S(2)}, u32[]{:S(2)}) async-start(bf16[4,4,16,3,256]{4,2,1,3,0:T(8,128)(2,1)} %copy.30), calls=%async_computation.2 | async-start | bytes 786432 | tf_op jit(solution)/shard_map/all_to_all | solution.py:159
  57.4 0.1 reshape.292
  57.5 0.1 select_reduce_fusion.3
  57.6 0.1 select_reduce_fusion.2
  57.8 11.4 %all-to-all-done.2 = bf16[4,4,16,3,256]{4,2,1,3,0:T(8,128)(2,1)S(1)} async-done(((bf16[4,4,16,3,256]{4,2,1,3,0:T(8,128)(2,1)}), bf16[4,4,16,3,256]{4,2,1,3,0:T(8,128)(2,1)S(1)}, u32[]{:S(2)}, u32[]{:S(2)}) %all-to-all-start.2) | async-done | bytes 393248 | tf_op jit(solution)/shard_map/all_to_all | solution.py:159
  69.2 0.8 copy.31
  70.0 3.5 %all-to-all-start.3 = ((bf16[4,4,16,3,256]{4,2,0,3,1:T(8,128)(2,1)}), bf16[4,4,16,3,256]{4,2,0,3,1:T(8,128)(2,1)S(1)}, u32[]{:S(2)}, u32[]{:S(2)}) async-start(bf16[4,4,16,3,256]{4,2,0,3,1:T(8,128)(2,1)} %copy.31), calls=%async_computation.3 | async-start | bytes 786432 | tf_op jit(solution)/shard_map/all_to_all | solution.py:158
  73.6 7.3 %all-to-all-done.3 = bf16[4,4,16,3,256]{4,2,0,3,1:T(8,128)(2,1)S(1)} async-done(((bf16[4,4,16,3,256]{4,2,0,3,1:T(8,128)(2,1)}), bf16[4,4,16,3,256]{4,2,0,3,1:T(8,128)(2,1)S(1)}, u32[]{:S(2)}, u32[]{:S(2)}) %all-to-all-start.3) | async-done | bytes 393248 | tf_op jit(solution)/shard_map/all_to_all | solution.py:158
  80.9 0.3 copy.33
  81.3 0.1 broadcast_in_dim.225
  81.4 7.0 %scatter_fusion = bf16[256,3,256]{2,1,0:T(4,128)(2,1)S(1)} fusion(bf16[256,3,256]{2,1,0:T(4,128)(2,1)S(1)} %broadcast_in_dim.225, s32[256]{0:T(256)S(1)} %bitcast.260, bf16[256,3,256]{2,1,0:T(4,128)(2,1)S(1)} %copy.33), kind=kCustom, calls=%fused_computation.4 | custom fusion | bytes 1180672 | tf_op jit(solution)/shard_map/scatter | solution.py:176
  88.4 0.5 fusion.89
  89.1 1.2 copy-done.7
  90.2 0.5 fusion.20
  90.7 0.5 copy-done.1
  91.2 0.2 copy-done.6
  91.3 0.8 fusion.8
  92.2 0.8 fusion.37
  93.0 3.8 %stack.135 = f32[6]{0:T(128)S(1)} concatenate(f32[1]{0:T(128)} %bitcast.30, f32[1]{0:T(128)} %bitcast.32, f32[1]{0:T(128)} %bitcast.34, f32[1]{0:T(128)} %bitcast.36, f32[1]{0:T(128)} %bitcast.38, f32[1]{0:T(128)} %bitcast.39), dimensions={0} | concatenate | bytes 48 | tf_op jit(solution)/shard_map/stack | solution.py:106
  96.8 5.7 %psum.28 = f32[6]{0:T(128)S(1)} all-reduce(f32[6]{0:T(128)S(1)} %stack.135), channel_id=1, replica_groups=mesh['groups'=2,'patch'=4,'sub'=2,'half'=2] {'sub','half'}, use_global_device_ids=true, to_apply=%region_9.11 | all-reduce | flops 6 | bytes 48 | tf_op jit(solution)/shard_map/psum | solution.py:208
  102.6 9.8 %psum.29 = f32[6]{0:T(128)S(1)} all-reduce(f32[6]{0:T(128)S(1)} %psum.28), channel_id=1, replica_groups=mesh['groups'=2,'patch'=4,'sub'=2,'half'=2] {'patch'}, use_global_device_ids=true, to_apply=%region_10.12 | all-reduce | flops 6 | bytes 48 | tf_op jit(solution)/shard_map/psum | solution.py:208
  112.4 0.7 fusion.91
  119.4 1.0 fusion.41
  120.4 0.2 add_multiply_fusion.5
  120.6 0.2 fusion.29
  120.9 0.9 copy-done.3
  121.9 0.2 multiply_add_fusion.1
  122.0 12.3 %gather_fusion.3 = f32[1024]{0:T(1024)S(1)} fusion(f32[2,2,128,256]{3,2,1,0:T(8,128)S(1)} %get-tuple-element.46, s32[1024]{0:T(1024)S(1)} %bitcast.213), kind=kCustom, calls=%fused_computation.3.clone | custom fusion | bytes 24576 | tf_op jit(solution)/shard_map/jit(take_along_axis)/gather | solution.py:72
  134.4 12.3 %gather_fusion.2 = f32[1024]{0:T(1024)S(1)} fusion(f32[2,2,128,256]{3,2,1,0:T(8,128)S(1)} %get-tuple-element.46, s32[1024]{0:T(1024)S(1)} %bitcast.211), kind=kCustom, calls=%fused_computation.2.clone | custom fusion | bytes 24576 | tf_op jit(solution)/shard_map/jit(take_along_axis)/gather | solution.py:72
  146.9 0.6 collective-permute-start.4
  147.5 3.3 %collective-permute-start.5 = (f32[2,2,2,2,256]{4,3,2,1,0:T(2,128)S(1)}, f32[2,2,2,2,256]{4,3,2,1,0:T(2,128)S(1)}, u32[]{:S(2)}, u32[]{:S(2)}) collective-permute-start(f32[2,2,2,2,256]{4,3,2,1,0:T(2,128)S(1)} %pad_maximum_fusion.5), channel_id=1, source_target_pairs={{0,12},{4,0},{8,4},{12,8},{1,13},{5,1},{9,5},{13,9},{2,14},{6,2},{... | collective-permute-start | bytes 49160 | tf_op jit(solution)/shard_map/ppermute | solution.py:15
  150.8 0.4 fusion.25
  151.1 0.2 add_multiply_fusion
  151.4 1.1 collective-permute-done.4
  152.5 0.1 select_reduce_fusion.1
  152.6 0.1 multiply_add_fusion.6
  152.8 0.1 select_reduce_fusion
  153.0 0.6 fusion.17
  153.6 0.3 copy-done.8
  154.0 0.8 fusion.33
  154.8 3.8 %stack.150 = f32[6]{0:T(128)S(1)} concatenate(f32[1]{0:T(128)} %bitcast.59, f32[1]{0:T(128)} %bitcast.61, f32[1]{0:T(128)} %bitcast.62, f32[1]{0:T(128)} %bitcast.64, f32[1]{0:T(128)} %bitcast.66, f32[1]{0:T(128)} %bitcast.67), dimensions={0} | concatenate | bytes 48 | tf_op jit(solution)/shard_map/stack | solution.py:106
  158.7 5.6 %psum.30 = f32[6]{0:T(128)S(1)} all-reduce(f32[6]{0:T(128)S(1)} %stack.150), channel_id=1, replica_groups=mesh['groups'=2,'patch'=4,'sub'=2,'half'=2] {'sub','half'}, use_global_device_ids=true, to_apply=%region_19.21 | all-reduce | flops 6 | bytes 48 | tf_op jit(solution)/shard_map/psum | solution.py:208
  164.3 12.2 %psum.31 = f32[6]{0:T(128)S(1)} all-reduce(f32[6]{0:T(128)S(1)} %psum.30), channel_id=1, replica_groups=mesh['groups'=2,'patch'=4,'sub'=2,'half'=2] {'patch'}, use_global_device_ids=true, to_apply=%region_20.22 | all-reduce | flops 6 | bytes 48 | tf_op jit(solution)/shard_map/psum | solution.py:208
  176.5 0.7 fusion.90
  183.7 0.2 add_multiply_fusion.3
  183.9 0.8 pad_maximum_fusion.1
  (92 shorter events, 1.7 us)
Async XLA Ops:
  0.0 0.7 copy-start.12
  27.1 30.4 %collective-permute-start.2 = (f32[2,2,2,2,256]{4,3,2,1,0:T(2,128)S(1)}, f32[2,2,2,2,256]{4,3,2,1,0:T(2,128)S(1)}, u32[]{:S(2)}, u32[]{:S(2)}) collective-permute-start(f32[2,2,2,2,256]{4,3,2,1,0:T(2,128)S(1)} %pad_maximum_fusion.4), channel_id=1, source_target_pairs={{0,4},{4,8},{8,12},{12,0},{1,5},{5,9},{9,13},{13,1},{2,6},{6,10},{... | collective-permute-start | bytes 49160 | tf_op jit(solution)/shard_map/ppermute | solution.py:15
  30.1 27.3 %collective-permute-start.3 = (f32[2,2,2,2,256]{4,3,2,1,0:T(2,128)S(1)}, f32[2,2,2,2,256]{4,3,2,1,0:T(2,128)S(1)}, u32[]{:S(2)}, u32[]{:S(2)}) collective-permute-start(f32[2,2,2,2,256]{4,3,2,1,0:T(2,128)S(1)} %pad_maximum_fusion.4), channel_id=1, source_target_pairs={{0,12},{4,0},{8,4},{12,8},{1,13},{5,1},{9,5},{13,9},{2,14},{6,2},{... | collective-permute-start | bytes 49160 | tf_op jit(solution)/shard_map/ppermute | solution.py:15
  32.2 0.7 copy-start.13
  32.9 3.9 %copy-start.11 = (s32[256]{0:T(256)S(1)}, s32[256]{0:T(256)}, u32[]{:S(2)}) copy-start(s32[256]{0:T(256)} %param.15) | copy-start | bytes 3076
  32.9 10.7 %collective-permute-start = (s32[2,2]{1,0:T(2,128)S(1)}, s32[2,2]{1,0:T(2,128)S(1)}, u32[]{:S(2)}, u32[]{:S(2)}) collective-permute-start(s32[2,2]{1,0:T(2,128)S(1)} %pad_add_fusion.4), channel_id=1, source_target_pairs={{0,4},{4,8},{8,12},{12,0},{1,5},{5,9},{9,13},{13,1},{2,6},{6,10},{... | collective-permute-start | bytes 56 | tf_op jit(solution)/shard_map/ppermute | solution.py:15
  33.0 10.6 %collective-permute-start.1 = (s32[2,2]{1,0:T(2,128)S(1)}, s32[2,2]{1,0:T(2,128)S(1)}, u32[]{:S(2)}, u32[]{:S(2)}) collective-permute-start(s32[2,2]{1,0:T(2,128)S(1)} %pad_add_fusion.4), channel_id=1, source_target_pairs={{0,12},{4,0},{8,4},{12,8},{1,13},{5,1},{9,5},{13,9},{2,14},{6,2},{... | collective-permute-start | bytes 56 | tf_op jit(solution)/shard_map/ppermute | solution.py:15
  37.5 8.8 %all-to-all-start = ((s32[4,4,16]{2,1,0:T(4,128)}), s32[4,4,16]{2,1,0:T(4,128)S(1)}, u32[]{:S(2)}, u32[]{:S(2)}) async-start(s32[4,4,16]{2,1,0:T(4,128)} %reshape.291), calls=%async_computation | async-start | bytes 16384 | tf_op jit(solution)/shard_map/all_to_all | solution.py:166
  40.8 1.1 copy-start
  41.8 1.0 copy-start.10
  46.9 7.0 %all-to-all-start.1 = ((s32[4,4,16]{2,0,1:T(4,128)}), s32[4,4,16]{2,0,1:T(4,128)S(1)}, u32[]{:S(2)}, u32[]{:S(2)}) async-start(s32[4,4,16]{2,0,1:T(4,128)} %copy.28), calls=%async_computation.1 | async-start | bytes 16384 | tf_op jit(solution)/shard_map/all_to_all | solution.py:165
  53.9 15.4 %all-to-all-start.2 = ((bf16[4,4,16,3,256]{4,2,1,3,0:T(8,128)(2,1)}), bf16[4,4,16,3,256]{4,2,1,3,0:T(8,128)(2,1)S(1)}, u32[]{:S(2)}, u32[]{:S(2)}) async-start(bf16[4,4,16,3,256]{4,2,1,3,0:T(8,128)(2,1)} %copy.30), calls=%async_computation.2 | async-start | bytes 786432 | tf_op jit(solution)/shard_map/all_to_all | solution.py:159
  70.0 10.9 %all-to-all-start.3 = ((bf16[4,4,16,3,256]{4,2,0,3,1:T(8,128)(2,1)}), bf16[4,4,16,3,256]{4,2,0,3,1:T(8,128)(2,1)S(1)}, u32[]{:S(2)}, u32[]{:S(2)}) async-start(bf16[4,4,16,3,256]{4,2,0,3,1:T(8,128)(2,1)} %copy.31), calls=%async_computation.3 | async-start | bytes 786432 | tf_op jit(solution)/shard_map/all_to_all | solution.py:158
  89.0 1.2 copy-start.7
  89.0 1.6 copy-start.2
  89.0 1.6 copy-start.4
  90.2 0.9 copy-start.1
  90.2 1.1 copy-start.6
  120.8 1.0 copy-start.3
  120.8 1.0 copy-start.5
  146.9 5.6 %collective-permute-start.4 = (f32[2,2,2,2,256]{4,3,2,1,0:T(2,128)S(1)}, f32[2,2,2,2,256]{4,3,2,1,0:T(2,128)S(1)}, u32[]{:S(2)}, u32[]{:S(2)}) collective-permute-start(f32[2,2,2,2,256]{4,3,2,1,0:T(2,128)S(1)} %pad_maximum_fusion.5), channel_id=1, source_target_pairs={{0,4},{4,8},{8,12},{12,0},{1,5},{5,9},{9,13},{13,1},{2,6},{6,10},{... | collective-permute-start | bytes 49160 | tf_op jit(solution)/shard_map/ppermute | solution.py:15
  147.5 5.0 %collective-permute-start.5 = (f32[2,2,2,2,256]{4,3,2,1,0:T(2,128)S(1)}, f32[2,2,2,2,256]{4,3,2,1,0:T(2,128)S(1)}, u32[]{:S(2)}, u32[]{:S(2)}) collective-permute-start(f32[2,2,2,2,256]{4,3,2,1,0:T(2,128)S(1)} %pad_maximum_fusion.5), channel_id=1, source_target_pairs={{0,12},{4,0},{8,4},{12,8},{1,13},{5,1},{9,5},{13,9},{2,14},{6,2},{... | collective-permute-start | bytes 49160 | tf_op jit(solution)/shard_map/ppermute | solution.py:15
  153.0 1.0 copy-start.8
  153.0 1.0 copy-start.9
